TPU v7x, 512 devices: a whole 4x8x8 slice. The times are simulated.
512 devices in a mesh: section: 4 (over x_hi, core), feat: 128 (over y, z, x_lo).
Axes of the slice: x: 4 (x_hi: 2, x_lo: 2; x = x_hi * 2 + x_lo), y: 8, z: 8, core: 2. Of those that a mesh axis runs over, the one named last changes fastest.
Arguments:
- inputs: bfloat16 [4, 128, 8192], P('section', None, 'feat'), may hold values from -6 to 6
- targets: bfloat16 [4, 128, 8192], P('section', None, 'feat'), may hold values from -6 to 6
- enc_w: bfloat16 [4, 4096, 8192], P('section', 'feat'), may hold values from -0.0625 to 0.0625
- enc_b: float32 [4, 4096], P('section', 'feat'), may hold values from -3 to 3
- dec_w: bfloat16 [4, 2, 8192, 4096], P('section', None, 'feat'), may hold values from -0.375 to 0.375
- dec_b: float32 [4, 8192], P('section', 'feat'), may hold values from -3 to 3
Outputs:
- enc_grad: bfloat16 [4, 4096, 8192], P('section', 'feat')
- dec_grad: bfloat16 [4, 2, 8192, 4096], P('section', None, 'feat')
All inputs are finite; a program needn't handle non-finite values.
Results may differ from a plain program's by a relative error of at most 0.0058.
Values may be sent and summed in bfloat16 or wider, within the bound.
A program may use at most 64 MiB of HBM per device.

v0:
```python
import jax
import jax.numpy as jnp
from jax import lax
from jax.sharding import PartitionSpec as P


def from_behind(value, axis, steps):
    count = lax.axis_size(axis)
    initial, last = (max(0, -steps), min(count, count - steps))
    return lax.ppermute(value, axis, [(source, source + steps) for source in range(initial, last)])


def transposed(left, right):
    return lax.dot_general(
        left, right, (((0,), (0,)), ((), ())), preferred_element_type=jnp.float32
    )


def against(left, right):
    return lax.dot_general(
        left, right, (((1,), (1,)), ((), ())), preferred_element_type=jnp.float32
    )


def on_device(inputs, targets, enc_w, enc_b, dec_w, dec_b):
    scale = inputs.shape[1] ** (-0.5)
    reach = dec_w.shape[1]
    gathered = lax.all_gather(inputs[0], "feat", axis=1, tiled=True)
    pre = against(gathered, enc_w[0]) + enc_b[0]
    active = jnp.maximum(pre, 0.0)
    codes = (active * active).astype(jnp.bfloat16)
    own_codes = lax.all_gather(codes, "feat", axis=1, tiled=True)
    target = targets[0].astype(jnp.float32)
    weights = dec_w[0]
    code_grad = None
    sources = [own_codes]
    previous = own_codes
    previous = from_behind(previous, "section", 1)
    sources.append(previous)
    total = dec_b[0] + against(sources[0], weights[0])
    offset = 1
    total = total + against(sources[offset], weights[offset])
    error = ((total - target) * scale).astype(jnp.bfloat16)
    slots = [transposed(error, sources[offset]).astype(jnp.bfloat16) for offset in range(reach)]
    code_grad = jnp.dot(error, weights[0], preferred_element_type=jnp.float32)
    held_error = error
    held_weights = weights[1:]
    held_error, held_weights = from_behind((held_error, held_weights), "section", -1)
    code_grad = code_grad + jnp.dot(held_error, held_weights[0], preferred_element_type=jnp.float32)
    mine = lax.psum_scatter(code_grad, "feat", scatter_dimension=1, tiled=True)
    pre_grad = (mine * 2.0 * active).astype(jnp.bfloat16)
    enc_grad = transposed(pre_grad, gathered).astype(jnp.bfloat16)[None]
    dec_grad = jnp.stack(slots)[None]
    return (enc_grad, dec_grad)


def solution(mesh):
    return jax.shard_map(
        on_device,
        mesh=mesh,
        in_specs=(
            P("section", None, "feat"),
            P("section", None, "feat"),
            P("section", "feat", None),
            P("section", "feat"),
            P("section", None, "feat", None),
            P("section", "feat"),
        ),
        out_specs=(P("section", "feat", None), P("section", None, "feat", None)),
        check_vma=False,
    )
```

profile of v0, /device:TPU:4, one launch (start us, length us, event | category | flops | bytes accessed | tf_op | source)
XLA Modules:
  0.0 1848.6 jit_solution(361580426507441476)
XLA Ops:
  7.2 0.0 copy-start
  7.2 0.0 copy-start.2
  7.2 0.0 copy-start.4
  7.2 0.0 all-gather.6.cloned.1.call-start
  7.2 0.7 all-gather.6.cloned.1.call-update
  7.9 0.0 all-gather.4.cloned.1.call-start
  8.0 596.3 %all-gather.6.cloned.1.call-done = bf16[1,128,8192]{1,2,0:T(8,128)(2,1)} async-done(((bf16[1,128,64]{1,2,0:T(8,128)(2,1)}), bf16[1,128,8192]{1,2,0:T(8,128)(2,1)}) %all-gather.6.cloned.1.call-update) | async-done | bytes 2097168 | tf_op jit(solution)/shard_map/all_gather | solution.py:28
  604.3 0.0 copy-done
  604.3 0.0 copy-start.3
  604.3 2.7 multiply_convert_fusion.1
  607.0 0.0 all-gather.4.cloned.1.call-update
  607.0 0.0 reduce-scatter.2.cloned.1.call-start
  607.0 582.7 %all-gather.4.cloned.1.call-done = bf16[128,4096]{0,1:T(8,128)(2,1)} async-done(((bf16[128,32]{0,1:T(8,128)(2,1)}), bf16[128,4096]{0,1:T(8,128)(2,1)}) %all-gather.4.cloned.1.call-update) | async-done | bytes 1048592 | tf_op jit(solution)/shard_map/all_gather | solution.py:32
  1189.7 1.9 collective-permute-start
  1191.7 0.0 copy-done.2
  1191.7 5.1 collective-permute-start.2
  1196.9 0.0 copy-done.4
  1196.9 1.5 convolution_add_fusion.2
  1198.4 9.1 collective-permute-done
  1207.6 0.0 copy-done.3
  1207.6 0.3 fusion.8
  1207.9 1.9 collective-permute-start.1
  1209.8 0.5 fusion.17
  1210.4 0.0 collective-permute-done.2
  1210.4 0.9 collective-permute-done.1
  1211.2 1.8 convolution_add_fusion
  1213.1 0.0 reduce-scatter.2.cloned.1.call-update
  1213.1 0.5 fusion.2
  1213.6 0.0 copy-start.1
  1213.6 1.9 fusion.1
  1215.5 1.1 maximum_bitcast_fusion
  1216.5 623.2 %reduce-scatter.2.cloned.1.call-done = f32[128,32]{0,1:T(8,128)} async-done(((f32[128,4096]{0,1:T(8,128)}), f32[128,32]{0,1:T(8,128)}) %reduce-scatter.2.cloned.1.call-update) | async-done | bytes 16400 | tf_op jit(solution)/shard_map/reduce_scatter | solution.py:50
  1839.7 0.0 copy-done.1
  1839.7 2.3 fusion
  (1 shorter events, 0.0 us)
Async XLA Ops:
  7.2 597.1 %copy-start = (bf16[1,32,8192]{2,1,0:T(8,128)(2,1)S(1)}, bf16[1,32,8192]{2,1,0:T(8,128)(2,1)}, u32[]{:S(2)}) copy-start(bf16[1,32,8192]{2,1,0:T(8,128)(2,1)} %param.8) | copy-start | bytes 1572868
  7.2 1184.5 %copy-start.2 = (bf16[1,2,64,4096]{3,2,1,0:T(8,128)(2,1)S(1)}, bf16[1,2,64,4096]{3,2,1,0:T(8,128)(2,1)}, u32[]{:S(2)}) copy-start(bf16[1,2,64,4096]{3,2,1,0:T(8,128)(2,1)} %param.10) | copy-start | bytes 3145732
  7.2 1189.7 %copy-start.4 = (f32[1,64]{1,0:T(1,128)S(1)}, f32[1,64]{1,0:T(1,128)}, u32[]{:S(2)}) copy-start(f32[1,64]{1,0:T(1,128)} %param.11) | copy-start | bytes 772
  7.2 597.1 %all-gather.6.cloned.1.call-start = ((), (), s32[]{:S(2)}) async-start(), calls=%async_computation.3 | async-start | bytes 2113536 | tf_op jit(solution)/shard_map/all_gather | solution.py:28
  7.9 1181.8 %all-gather.4.cloned.1.call-start = ((), (), s32[]{:S(2)}) async-start(), calls=%async_computation.1 | async-start | bytes 1056768 | tf_op jit(solution)/shard_map/all_gather | solution.py:32
  604.3 603.3 %copy-start.3 = (bf16[1,128,64]{1,2,0:T(8,128)(2,1)S(1)}, bf16[1,128,64]{1,2,0:T(8,128)(2,1)}, u32[]{:S(2)}) copy-start(bf16[1,128,64]{1,2,0:T(8,128)(2,1)} %param.7) | copy-start | bytes 49156
  607.0 1232.7 %reduce-scatter.2.cloned.1.call-start = ((), (), s32[]{:S(2)}) async-start(), calls=%async_computation.2 | async-start | bytes 2113536 | tf_op jit(solution)/shard_map/reduce_scatter | solution.py:50
  1189.7 17.8 collective-permute-start
  1191.7 18.6 %collective-permute-start.2 = (bf16[1,64,4096]{2,1,0:T(8,128)(2,1)S(1)}, bf16[1,64,4096]{2,1,0:T(8,128)(2,1)S(1)}, u32[]{:S(2)}, u32[]{:S(2)}) collective-permute-start(bf16[1,64,4096]{2,1,0:T(8,128)(2,1)S(1)} %slice_bitcast_fusion), channel_id=1, source_target_pairs={{128,0},{256,128},{384,256},{129,1},{257,129},{385,257},{130,2},{2... | collective-permute-start | bytes 1572872 | tf_op jit(solution)/shard_map/ppermute | solution.py:10
  1207.9 3.4 collective-permute-start.1
  1213.6 626.2 %copy-start.1 = (bf16[1,128,8192]{1,2,0:T(8,128)(2,1)S(1)}, bf16[1,128,8192]{1,2,0:T(8,128)(2,1)}, u32[]{:S(2)}) copy-start(bf16[1,128,8192]{1,2,0:T(8,128)(2,1)} %all-gather.6.cloned.1.call-done) | copy-start | bytes 6291460
Sparse Core Ops, SparseCore 0:
  10.1 594.1 all-gather.5
  607.1 582.5 all-gather.3
  1213.2 626.4 reduce-scatter.1
where the time goes:
time: 1850 us
  waiting for transfers between devices  1810 us (98%)
    reduce_scatter x1, waiting for transfers between devices, on_device(): mine = lax.psum_scatter(code_grad, 'feat', scatter_dimension=1, tiled=True)  623 us
    all_gather x1, waiting for transfers between devices, on_device(): gathered = lax.all_gather(inputs[0], 'feat', axis=1, tiled=True)  596 us
    all_gather x1, waiting for transfers between devices, on_device(): own_codes = lax.all_gather(codes, 'feat', axis=1, tiled=True)  583 us
  transfers between devices with their start and end apart: 6, of which 5 were waited for; matrix products, arithmetic and copies ran while one was open for 0% of the time, Pallas kernels for 0%

commit v1 on v0

v1 whole, which is shorter than its diff:
```python
import functools

import jax
import jax.numpy as jnp
from jax import lax
from jax.experimental import pallas as pl
from jax.experimental.pallas import tpu as pltpu
from jax.sharding import PartitionSpec as P

MESH = pl.DeviceIdType.MESH
NY, NZ, NX = 8, 8, 2
BF16, F32 = jnp.bfloat16, jnp.float32


def mod(a, n):
    return lax.rem(a + n, n)


def dot(a, b):
    return jnp.dot(a, b, preferred_element_type=F32)


def dot_nt(a, b):
    return lax.dot_general(a, b, (((1,), (1,)), ((), ())), preferred_element_type=F32)


def column(row):
    n = row.shape[1]
    here = lax.broadcasted_iota(jnp.int32, (n, n), 0) == lax.broadcasted_iota(jnp.int32, (n, n), 1)
    return jnp.sum(jnp.where(here, jnp.broadcast_to(row, (n, n)), 0.0), axis=1, keepdims=True)


def kernel(
    scale, in_ref, tgt_ref, encw_hbm, encb_ref, decw_hbm, decb_ref,
    eg_ref, dg_ref,
    gin, cod, cprev, encw, decw, dwn, wt, err, rprev, rsend, active, part, one_in, two_in, two_out, x_in, x_out,
    load_sem, s_x, r_x, s_one, r_one, s_ring, r_ring, s_sec, r_sec, s_r1, r_r1, s_r2, r_r2,
):
    s = lax.axis_index("section")
    f = lax.axis_index("feat")
    xl = lax.rem(f, NX)
    z = lax.rem(f // NX, NZ)
    y = f // (NX * NZ)

    def at(yy, zz, xx):
        return {"section": s, "feat": (yy * NZ + zz) * NX + xx}

    mate = at(y, z, 1 - xl)
    far_f = (y * NZ + z) * NX + 1 - xl
    odd = lax.rem(s, 2)
    up = {"section": jnp.minimum(s + 1, 3), "feat": jnp.where(odd == 1, far_f, f)}
    down = {"section": jnp.maximum(s - 1, 0), "feat": jnp.where(odd == 0, far_f, f)}
    has_up = s < 3
    has_down = s > 0

    load_e = pltpu.make_async_copy(encw_hbm, encw, load_sem.at[0])
    load_d = pltpu.make_async_copy(decw_hbm, decw, load_sem.at[1])
    load_e.start()
    load_d.start()

    barrier = pltpu.get_barrier_semaphore()
    for j in range(1, NY):
        pl.semaphore_signal(barrier, inc=1, device_id=at(mod(y + j, NY), z, xl), device_id_type=MESH)
    for j in range(1, NZ):
        pl.semaphore_signal(barrier, inc=1, device_id=at(y, mod(z + j, NZ), xl), device_id_type=MESH)
    pl.semaphore_signal(barrier, inc=1, device_id=mate, device_id_type=MESH)

    @pl.when(has_up)
    def _():
        pl.semaphore_signal(barrier, inc=1, device_id=up, device_id_type=MESH)

    @pl.when(has_down)
    def _():
        pl.semaphore_signal(barrier, inc=1, device_id=down, device_id_type=MESH)

    pl.semaphore_wait(barrier, NY + NZ - 1 + jnp.where(has_up, 1, 0) + jnp.where(has_down, 1, 0))

    def remote(src, dst, ss, rs, to):
        return pltpu.make_async_remote_copy(
            src_ref=src, dst_ref=dst, send_sem=ss, recv_sem=rs, device_id=to, device_id_type=MESH
        )

    def slab(buf, c, i, h):
        half = pl.ds(4 * h, 4)
        return buf.at[i, half, 0] if c == 0 else buf.at[half, i, 1]

    def ring_copy(buf, g, c, d, k, h, i):
        step = 1 if d == 0 else -1
        to = at(mod(y + step, NY), z, xl) if c == 0 else at(y, mod(z + step, NZ), xl)
        return remote(slab(buf, c, i, h), slab(buf, c, i, h), s_ring.at[g, c, d, k, h], r_ring.at[g, c, d, k, h], to)

    def gather_start(buf, g):
        own = remote(buf.at[y, z, xl], buf.at[y, z, xl], s_x.at[g], r_x.at[g], mate)
        own.start()

        def line(c):
            copies = []
            for j in range(1, 8):
                to = at(mod(y + j * c, NY), mod(z + j * (1 - c), NZ), xl)
                copies.append(remote(buf.at[y, z, c], buf.at[y, z, c], s_one.at[g, c, j], r_one.at[g, c, j], to))
            for copy in copies:
                copy.start()
            return copies

        first = line(xl)
        own.wait_recv()
        second = line(1 - xl)
        return own, first, second

    def gather_rest(buf, g, own, first, second):
        for copy in first + second:
            copy.wait_recv()
        sent = []
        for c in range(2):
            for h in range(2):
                for d in range(2):
                    copy = ring_copy(buf, g, c, d, 1, h, y if c == 0 else z)
                    copy.start()
                    sent.append(copy)
        for k in range(1, 5):
            for h in range(2):
                for c in range(2):
                    for d in range(2):
                        if k == 4 and h != d:
                            continue
                        step = 1 if d == 0 else -1
                        i = mod((y if c == 0 else z) - step * k, 8)
                        ring_copy(buf, g, c, d, k, h, i).wait_recv()
                        if k < 3 or (k == 3 and h == d):
                            copy = ring_copy(buf, g, c, d, k + 1, h, i)
                            copy.start()
                            sent.append(copy)
        return [own] + first + second + sent

    gin[y, z, xl] = in_ref[...]
    state = gather_start(gin, 0)
    load_e.wait()
    load_d.wait()

    send_w = remote(decw.at[1], dwn, s_sec.at[0], r_sec.at[0], down)

    @pl.when(has_down)
    def _():
        send_w.start()

    sent = gather_rest(gin, 0, *state)

    def pre_step(i, acc):
        return acc + dot(encw[:, pl.ds(pl.multiple_of(i * 1024, 1024), 1024)], gin[i].reshape(1024, 128))

    pre = lax.fori_loop(0, NY, pre_step, jnp.zeros((32, 128), F32)) + column(encb_ref[...])
    act = jnp.maximum(pre, 0.0)
    active[...] = act
    cod[y, z, xl] = (act * act).astype(BF16)
    state = gather_start(cod, 1)

    @pl.when(has_up)
    def _():
        send_w.wait_recv()

    @pl.when(jnp.logical_not(has_up))
    def _():
        dwn[...] = jnp.zeros_like(dwn)
        err[pl.ds(64, 64), :] = jnp.zeros((64, 128), BF16)

    sent += gather_rest(cod, 1, *state)

    def through(weights):
        def step(i, acc):
            return acc + dot(weights[:, pl.ds(pl.multiple_of(i * 512, 512), 512)], cod[i].reshape(512, 128))

        return lax.fori_loop(0, NY, step, jnp.zeros((64, 128), F32))

    send_r = remote(rsend, rprev, s_sec.at[1], r_sec.at[1], up)
    send_c = remote(cod, cprev, s_sec.at[2], r_sec.at[2], up)
    send_e = remote(err.at[pl.ds(0, 64)], err.at[pl.ds(64, 64)], s_sec.at[3], r_sec.at[3], down)

    @pl.when(has_up)
    def _():
        rsend[...] = through(dwn)
        send_r.start()
        send_c.start()

    @pl.when(jnp.logical_not(has_down))
    def _():
        rprev[...] = jnp.zeros_like(rprev)

    total = through(decw.at[0]) + column(decb_ref[...])

    @pl.when(has_down)
    def _():
        send_r.wait_recv()

    total = total + rprev[...]
    err[pl.ds(0, 64), :] = ((total - tgt_ref[...].astype(F32)) * scale).astype(BF16)

    @pl.when(has_down)
    def _():
        send_e.start()

    def decoder_grad(slot, codes):
        def step(i, carry):
            block = dot_nt(err[pl.ds(0, 64), :], codes[i].reshape(512, 128))
            dg_ref[slot, :, pl.ds(pl.multiple_of(i * 512, 512), 512)] = block.astype(BF16)
            return carry

        lax.fori_loop(0, NY, step, 0)

    decoder_grad(0, cod)

    @pl.when(has_up)
    def _():
        send_e.wait_recv()

    def grad_step(i, carry):
        cols = pl.ds(pl.multiple_of(i * 512, 512), 512)
        both = jnp.concatenate([decw[0, :, cols], dwn[:, cols]], axis=0)
        block = lax.dot_general(both, err[...], (((0,), (0,)), ((), ())), preferred_element_type=F32)
        part[i] = block.astype(BF16).reshape(NZ, NX, 32, 128)
        return carry

    lax.fori_loop(0, NY, grad_step, 0)

    ones = []
    for j in range(1, 8):
        yy, zz = mod(y + j, NY), mod(z + j, NZ)
        ones.append(remote(part.at[yy, :, 0], one_in.at[0, j], s_r1.at[0, j], r_r1.at[0, j], at(yy, z, xl)))
        ones.append(remote(part.at[:, zz, 1], one_in.at[1, j], s_r1.at[1, j], r_r1.at[1, j], at(y, zz, xl)))
    for copy in ones:
        copy.start()

    @pl.when(has_down)
    def _():
        send_c.wait_recv()
        decoder_grad(1, cprev)

    @pl.when(jnp.logical_not(has_down))
    def _():
        dg_ref[1] = jnp.zeros((64, 4096), BF16)

    for copy in ones:
        copy.wait_recv()

    def sum_one(c):
        own = part[y, :, 0] if c == 0 else part[:, z, 1]
        acc = own.astype(F32)
        for j in range(1, 8):
            acc = acc + one_in[c, j].astype(F32)
        return acc

    for c in range(2):
        two_out[c] = sum_one(c).astype(BF16)
    twos = []
    for j in range(1, 8):
        yy, zz = mod(y + j, NY), mod(z + j, NZ)
        twos.append(remote(two_out.at[0, zz], two_in.at[0, j], s_r2.at[0, j], r_r2.at[0, j], at(y, zz, xl)))
        twos.append(remote(two_out.at[1, yy], two_in.at[1, j], s_r2.at[1, j], r_r2.at[1, j], at(yy, z, xl)))
    for copy in twos:
        copy.start()
    for copy in twos:
        copy.wait_recv()
    acc0 = two_out[0, z].astype(F32)
    acc1 = two_out[1, y].astype(F32)
    for j in range(1, 8):
        acc0 = acc0 + two_in[0, j].astype(F32)
        acc1 = acc1 + two_in[1, j].astype(F32)
    x_out[...] = jnp.where(xl == 0, acc1, acc0)
    last = remote(x_out, x_in, s_x.at[2], r_x.at[2], mate)
    last.start()
    mine = jnp.where(xl == 0, acc0, acc1)
    last.wait_recv()
    mine = mine + x_in[...]

    pre_grad = (mine * 2.0 * active[...]).astype(BF16)

    def enc_step(i, carry):
        block = dot_nt(pre_grad, gin[i].reshape(1024, 128))
        eg_ref[:, pl.ds(pl.multiple_of(i * 1024, 1024), 1024)] = block.astype(BF16)
        return carry

    lax.fori_loop(0, NY, enc_step, 0)

    for copy in sent + ones + twos + [last]:
        copy.wait_send()

    @pl.when(has_down)
    def _():
        send_w.wait_send()
        send_e.wait_send()

    @pl.when(has_up)
    def _():
        send_r.wait_send()
        send_c.wait_send()


def on_device(inputs, targets, enc_w, enc_b, dec_w, dec_b):
    scale = inputs.shape[1] ** (-0.5)
    vmem = pl.BlockSpec(memory_space=pltpu.VMEM)
    hbm = pl.BlockSpec(memory_space=pl.ANY)
    dma = pltpu.SemaphoreType.DMA
    grid = (NY, NZ, NX, 32, 128)
    eg, dg = pl.pallas_call(
        functools.partial(kernel, scale),
        out_shape=(
            jax.ShapeDtypeStruct((32, 8192), BF16),
            jax.ShapeDtypeStruct((2, 64, 4096), BF16),
        ),
        in_specs=[vmem, vmem, hbm, vmem, hbm, vmem],
        out_specs=(vmem, vmem),
        scratch_shapes=[
            pltpu.VMEM((NY, NZ, NX, 64, 128), BF16),
            pltpu.VMEM(grid, BF16),
            pltpu.VMEM(grid, BF16),
            pltpu.VMEM((32, 8192), BF16),
            pltpu.VMEM((2, 64, 4096), BF16),
            pltpu.VMEM((64, 4096), BF16),
            pltpu.VMEM((8, 128), BF16),
            pltpu.VMEM((128, 128), BF16),
            pltpu.VMEM((64, 128), F32),
            pltpu.VMEM((64, 128), F32),
            pltpu.VMEM((32, 128), F32),
            pltpu.VMEM(grid, BF16),
            pltpu.VMEM((2, 8, 8, 32, 128), BF16),
            pltpu.VMEM((2, 8, 32, 128), BF16),
            pltpu.VMEM((2, 8, 32, 128), BF16),
            pltpu.VMEM((32, 128), F32),
            pltpu.VMEM((32, 128), F32),
            dma((2,)),
            dma((3,)),
            dma((3,)),
            dma((2, 2, 8)),
            dma((2, 2, 8)),
            dma((2, 2, 2, 5, 2)),
            dma((2, 2, 2, 5, 2)),
            dma((4,)),
            dma((4,)),
            dma((2, 8)),
            dma((2, 8)),
            dma((2, 8)),
            dma((2, 8)),
        ],
        compiler_params=pltpu.CompilerParams(collective_id=0, has_side_effects=True),
    )(inputs[0].T, targets[0].T, enc_w[0], enc_b, dec_w[0], dec_b)
    return eg[None], dg[None]


def solution(mesh):
    return jax.shard_map(
        on_device,
        mesh=mesh,
        in_specs=(
            P("section", None, "feat"),
            P("section", None, "feat"),
            P("section", "feat", None),
            P("section", "feat"),
            P("section", None, "feat", None),
            P("section", "feat"),
        ),
        out_specs=(P("section", "feat", None), P("section", None, "feat", None)),
        check_vma=False,
    )
```

time: 1850 us -> 101 us (0.05)
  the two profiles are of different devices: /device:TPU:4 before, /device:TPU:1 now
where the time goes in v1:
time: 101 us; the launch traced here: 100 us
  Pallas kernels  96.8 us (96%)
  local copies, waits for them, and re-layouts  2.93 us (3%)
    pallas_call x1, Pallas kernels, on_device(): pl.pallas_call(functools.partial(kernel, scale), out_shape=(jax.ShapeDtyp...  96.8 us
    unnamed x4, local copies, waits for them, and re-layouts  2.93 us

profile of v1, /device:TPU:1, one launch (start us, length us, event | category | flops | bytes accessed | tf_op | source)
XLA Modules:
  0.0 100.4 jit_solution(3550302152666655616)
XLA Ops:
  0.6 96.8 %shard_map.77 = (bf16[32,8192]{1,0:T(8,128)(2,1)}, bf16[2,64,4096]{2,1,0:T(8,128)(2,1)}) custom-call(bf16[64,128]{1,0:T(8,128)(2,1)} %bitcast.14, bf16[64,128]{1,0:T(8,128)(2,1)} %bitcast.15, bf16[32,8192]{1,0:T(8,128)(2,1)} %bitcast.13, f32[1,32]{1,0:T(1,128)} %encb_ref.1, bf16[2,64,4096]{2,1,0:T(8,128)(2,1)} %bitcast.10, f32[1,64]{1,0:T(1,128)} %decb_ref.1), custom_call_target="tpu_custom_call" | custom-call | tf_op jit(solution)/shard_map/pallas_call | solution.py:303
  97.4 0.0 copy-start
  97.4 2.0 %copy.10 = bf16[1,32,8192]{2,1,0:T(8,128)(2,1)} copy(bf16[1,32,8192]{2,1,0:T(8,128)(2,1)} %bitcast.12) | data formatting | bytes 1048576
  99.4 0.0 copy-done
  99.4 1.0 copy.11
Async XLA Ops:
  97.4 2.0 %copy-start = (bf16[2,64,4096]{2,1,0:T(8,128)(2,1)S(1)}, bf16[2,64,4096]{2,1,0:T(8,128)(2,1)}, u32[]{:S(2)}) copy-start(bf16[2,64,4096]{2,1,0:T(8,128)(2,1)} %get-tuple-element.5) | copy-start | bytes 3145732

commit v2 on v1

v2 whole, which is shorter than its diff:
```python
import functools

import jax
import jax.numpy as jnp
from jax import lax
from jax.experimental import pallas as pl
from jax.experimental.pallas import tpu as pltpu
from jax.sharding import PartitionSpec as P

MESH = pl.DeviceIdType.MESH
NY, NZ, NX = 8, 8, 2
BF16, F32 = jnp.bfloat16, jnp.float32


def mod(a, n):
    return lax.rem(a + n, n)


def dot(a, b):
    return jnp.dot(a, b, preferred_element_type=F32)


def dot_nt(a, b):
    return lax.dot_general(a, b, (((1,), (1,)), ((), ())), preferred_element_type=F32)


def column(row):
    n = row.shape[1]
    here = lax.broadcasted_iota(jnp.int32, (n, n), 0) == lax.broadcasted_iota(jnp.int32, (n, n), 1)
    return jnp.sum(jnp.where(here, jnp.broadcast_to(row, (n, n)), 0.0), axis=1, keepdims=True)


GROUPS = ((0, 1, -1), (2, -2), (3, -3, 4))
OFFS = tuple(o for group in GROUPS for o in group)


def group_of(o):
    return next(n for n, group in enumerate(GROUPS) if o in group)


def back(o):
    return o if o == 4 else -o


def reach(d, o):
    return 4 if OFFS.index(o) % 2 == d else 3


def travellers(n, d, k):
    return [o for o in GROUPS[n] if k <= reach(d, o)]


PIECES = (4, 4)


def ring_order(g):
    pieces = PIECES[g]
    return [
        (k, h, role, d)
        for k in range(1, 5) for h in range(pieces) for role in range(2) for d in range(2)
        if k < 4 or h // (pieces // 2) == d
    ]


def kernel(
    scale, in_hbm, tgt_hbm, encw_hbm, encb_hbm, decw_hbm, decb_hbm,
    eg_hbm, dg_hbm,
    eg_ref, dg_ref, out_sem, gin, cod, cprev, cown, tgt, encb_ref, decb_ref, encw, decw, dwn, err, rprev, rsend, active, part, ring_in, ring_out, two_in, two_out,
    load_sem, s_line, r_one, s_ring, r_ring, s_sec, r_sec, s_red, r_red, s_two, r_two,
):
    s = lax.axis_index("section")
    f = lax.axis_index("feat")
    xl = lax.rem(f, NX)
    z = lax.rem(f // NX, NZ)
    y = f // (NX * NZ)
    ys = {o: mod(y + o, NY) for o in range(-4, 5)}
    zs = {o: mod(z + o, NZ) for o in range(-4, 5)}

    def at(yy, zz, xx):
        return {"section": s, "feat": (yy * NZ + zz) * NX + xx}

    far_f = (y * NZ + z) * NX + 1 - xl
    odd = lax.rem(s, 2)
    up = {"section": jnp.minimum(s + 1, 3), "feat": jnp.where(odd == 1, far_f, f)}
    down = {"section": jnp.maximum(s - 1, 0), "feat": jnp.where(odd == 0, far_f, f)}
    has_up = s < 3
    has_down = s > 0

    even = xl == 0
    ring = [{o: jnp.where(even, ys[o], zs[o]) for o in ys}, {o: jnp.where(even, zs[o], ys[o]) for o in ys}]
    line = ring[::-1]
    colour = [xl, 1 - xl]

    def along_ring(role, o, xx):
        if role == 0:
            return at(jnp.where(even, ys[o], y), jnp.where(even, z, zs[o]), xx)
        return at(jnp.where(even, y, ys[o]), jnp.where(even, zs[o], z), xx)

    mate = at(y, z, 1 - xl)
    barrier = pltpu.get_barrier_semaphore()
    for o in OFFS:
        if o != 0:
            pl.semaphore_signal(barrier, inc=1, device_id=at(ys[o], z, xl), device_id_type=MESH)
            pl.semaphore_signal(barrier, inc=1, device_id=at(y, zs[o], xl), device_id_type=MESH)
        pl.semaphore_signal(barrier, inc=1, device_id=along_ring(1, o, 1 - xl), device_id_type=MESH)

    @pl.when(has_up)
    def _():
        pl.semaphore_signal(barrier, inc=1, device_id=up, device_id_type=MESH)

    @pl.when(has_down)
    def _():
        pl.semaphore_signal(barrier, inc=1, device_id=down, device_id_type=MESH)

    load_e = pltpu.make_async_copy(encw_hbm, encw, load_sem.at[0])
    load_d = pltpu.make_async_copy(decw_hbm, decw, load_sem.at[1])
    load_t = pltpu.make_async_copy(tgt_hbm, tgt, load_sem.at[2])
    load_b = pltpu.make_async_copy(encb_hbm, encb_ref, load_sem.at[3])
    load_c = pltpu.make_async_copy(decb_hbm, decb_ref, load_sem.at[4])
    for load in (load_d, load_e, load_t, load_b, load_c):
        load.start()

    pl.semaphore_wait(barrier, 22 + jnp.where(has_up, 1, 0) + jnp.where(has_down, 1, 0))

    def remote(src, dst, ss, rs, to):
        return pltpu.make_async_remote_copy(
            src_ref=src, dst_ref=dst, send_sem=ss, recv_sem=rs, device_id=to, device_id_type=MESH
        )

    def arrived(blocks, sem):
        pltpu.make_async_copy(blocks, blocks, sem).wait()

    def place(buf, role, i, o):
        return buf.at[colour[role], ring[role][i], line[role][o]]

    def gather(buf, g, src):
        own = place(buf, 0, 0, 0)
        pltpu.make_async_copy(src, own, r_one.at[g, 0]).start()
        remote(src, own, s_line.at[g], r_one.at[g, 2], mate).start()
        for o in reversed(OFFS):
            if o != 0:
                remote(src, own, s_line.at[g], r_one.at[g, 0], along_ring(1, o, xl)).start()
        other = place(buf, 1, 0, 0)
        arrived(other, r_one.at[g, 2])
        for o in reversed(OFFS):
            if o != 0:
                remote(other, other, s_line.at[g], r_one.at[g, 1], along_ring(0, o, xl)).start()

    def gather_rest(buf, g):
        blocks = 8 // PIECES[g]

        def piece(role, i, h):
            return buf.at[colour[role], ring[role][i], pl.ds(h * blocks, blocks)]

        def send(role, d, k, h):
            ref = piece(role, 1 - k if d == 0 else k - 1, h)
            to = along_ring(role, 1 if d == 0 else -1, xl)
            remote(ref, ref, s_ring.at[g], r_ring.at[g, role, d, k - 1, h], to).start()

        for role in range(2):
            arrived(buf.at[0, 0, pl.ds(0, 8 - role)], r_one.at[g, role])
            for h in range(PIECES[g]):
                for d in range(2):
                    send(role, d, 1, h)
        for k, h, role, d in ring_order(g):
            arrived(piece(role, -k if d == 0 else k, h), r_ring.at[g, role, d, k - 1, h])
            if (k + 1, h, role, d) in ring_order(g):
                send(role, d, k + 1, h)

    def rows_of(buf, i):
        both = jnp.stack([buf[0, i], buf[1, :, i]], axis=1)
        return both.reshape(-1, 128)

    gather(gin, 0, in_hbm)
    load_d.wait()
    send_w = remote(decw.at[1], dwn, s_sec.at[0], r_sec.at[0], down)

    @pl.when(has_down)
    def _():
        send_w.start()

    for load in (load_e, load_t, load_b, load_c):
        load.wait()
    gather_rest(gin, 0)

    def pre_step(i, acc):
        return acc + dot(encw[:, pl.ds(pl.multiple_of(i * 1024, 1024), 1024)], rows_of(gin, i))

    pre = lax.fori_loop(0, NY, pre_step, jnp.zeros((32, 128), F32)) + column(encb_ref[...])
    act = jnp.maximum(pre, 0.0)
    active[...] = act
    cown[...] = (act * act).astype(BF16)
    gather(cod, 1, cown)

    @pl.when(has_up)
    def _():
        send_w.wait_recv()

    @pl.when(jnp.logical_not(has_up))
    def _():
        dwn[...] = jnp.zeros_like(dwn)
        err[pl.ds(64, 64), :] = jnp.zeros((64, 128), BF16)

    gather_rest(cod, 1)

    def through(weights):
        def step(i, acc):
            return acc + dot(weights[:, pl.ds(pl.multiple_of(i * 512, 512), 512)], rows_of(cod, i))

        return lax.fori_loop(0, NY, step, jnp.zeros((64, 128), F32))

    send_r = remote(rsend, rprev, s_sec.at[1], r_sec.at[1], up)
    send_c = remote(cod, cprev, s_sec.at[2], r_sec.at[2], up)
    send_e = remote(err.at[pl.ds(0, 64)], err.at[pl.ds(64, 64)], s_sec.at[3], r_sec.at[3], down)

    @pl.when(has_up)
    def _():
        rsend[...] = through(dwn)
        send_r.start()
        send_c.start()

    @pl.when(jnp.logical_not(has_down))
    def _():
        rprev[...] = jnp.zeros_like(rprev)

    total = through(decw.at[0]) + column(decb_ref[...])

    @pl.when(has_down)
    def _():
        send_r.wait_recv()

    total = total + rprev[...]
    err[pl.ds(0, 64), :] = ((total - tgt[...].astype(F32)) * scale).astype(BF16)

    @pl.when(has_down)
    def _():
        send_e.start()

    def decoder_grad(slot, codes):
        def step(i, carry):
            block = dot_nt(err[pl.ds(0, 64), :], rows_of(codes, i))
            dg_ref[slot, :, pl.ds(pl.multiple_of(i * 512, 512), 512)] = block.astype(BF16)
            return carry

        lax.fori_loop(0, NY, step, 0)

    decoder_grad(0, cod)
    out_0 = pltpu.make_async_copy(dg_ref.at[0], dg_hbm.at[0], out_sem.at[0])
    out_0.start()

    @pl.when(has_up)
    def _():
        send_e.wait_recv()

    def grad_step(i, carry):
        cols = pl.ds(pl.multiple_of(i * 512, 512), 512)
        both = jnp.concatenate([decw[0, :, cols], dwn[:, cols]], axis=0)
        block = lax.dot_general(both, err[...], (((0,), (0,)), ((), ())), preferred_element_type=F32)
        block = block.reshape(NZ, NX, 32, 128)
        part[0, i] = block[:, 0]
        part[1, :, i] = block[:, 1]
        return carry

    lax.fori_loop(0, NY, grad_step, 0)

    def own_part(c, i, o):
        return part[0, ys[i], zs[o]] if c == 0 else part[1, zs[i], ys[o]]

    def ring_to(c, d):
        step = 1 if d == 0 else -1
        return at(ys[step], z, xl) if c == 0 else at(y, zs[step], xl)

    for m in (4, 3, 2, 1):
        for n in reversed(range(len(GROUPS))):
            for c in range(2):
                for d in range(2):
                    passing = travellers(n, d, m + 1)
                    if passing:
                        arrived(ring_in.at[c, d, m, pl.ds(0, len(passing))], r_red.at[c, d, m, n])
                    for o in travellers(n, d, m):
                        slot = OFFS.index(o)
                        value = own_part(c, m if d == 0 else -m, o)
                        if o in passing:
                            value = value + ring_in[c, d, m, slot].astype(F32)
                        ring_out[c, d, m - 1, slot] = value.astype(BF16)
                        remote(
                            ring_out.at[c, d, m - 1, slot], ring_in.at[c, d, m - 1, slot], s_red,
                            r_red.at[c, d, m - 1, n], ring_to(c, d),
                        ).start()

    for n in reversed(range(len(GROUPS))):
        for c in range(2):
            for d in range(2):
                arrived(ring_in.at[c, d, 0, pl.ds(0, len(GROUPS[n]))], r_red.at[c, d, 0, n])
            for o in GROUPS[n]:
                slot = OFFS.index(o)
                value = own_part(c, 0, o)
                for d in range(2):
                    value = value + ring_in[c, d, 0, slot].astype(F32)
                two_out[c, slot] = value.astype(BF16)
                to = at(y, zs[o], 0) if c == 0 else at(ys[o], z, 1)
                send_two = remote(two_out.at[c, slot], two_in.at[xl, OFFS.index(back(o))], s_two, r_two, to)
                if o != 0:
                    send_two.start()
                else:
                    pl.when(xl != c)(send_two.start)

    @pl.when(has_down)
    def _():
        send_c.wait_recv()
        decoder_grad(1, cprev)

    @pl.when(jnp.logical_not(has_down))
    def _():
        dg_ref[1] = jnp.zeros((64, 4096), BF16)

    out_1 = pltpu.make_async_copy(dg_ref.at[1], dg_hbm.at[1], out_sem.at[1])
    out_1.start()
    arrived(cprev.at[0, pl.ds(0, 5), pl.ds(0, 3)], r_two)
    mine = two_out[xl, 0].astype(F32) + two_in[1 - xl, 0].astype(F32)
    for o in OFFS[1:]:
        slot = OFFS.index(o)
        mine = mine + two_in[0, slot].astype(F32) + two_in[1, slot].astype(F32)

    pre_grad = (mine * 2.0 * active[...]).astype(BF16)

    def enc_step(i, carry):
        block = dot_nt(pre_grad, rows_of(gin, i))
        cols = pl.ds(pl.multiple_of(i * 1024, 1024), 1024)
        eg_ref[:, cols] = block.astype(BF16)
        pltpu.make_async_copy(eg_ref.at[:, cols], eg_hbm.at[:, cols], out_sem.at[2]).start()
        return carry

    lax.fori_loop(0, NY, enc_step, 0)

    pltpu.make_async_copy(eg_ref, eg_hbm, out_sem.at[2]).wait()
    out_0.wait()
    out_1.wait()
    for g, buf in enumerate((gin, cod)):
        arrived(buf.at[0, pl.ds(0, 5), pl.ds(0, 3)], s_line.at[g])
        arrived(buf.at[:, pl.ds(0, 7)], s_ring.at[g])
    arrived(ring_out.at[:, :, :, pl.ds(0, 7)], s_red)
    arrived(cprev.at[0, pl.ds(0, 5), pl.ds(0, 3)], s_two)

    @pl.when(has_down)
    def _():
        send_w.wait_send()
        send_e.wait_send()

    @pl.when(has_up)
    def _():
        send_r.wait_send()
        send_c.wait_send()


def on_device(inputs, targets, enc_w, enc_b, dec_w, dec_b):
    scale = inputs.shape[1] ** (-0.5)
    vmem = pl.BlockSpec(memory_space=pltpu.VMEM)
    hbm = pl.BlockSpec(memory_space=pltpu.HBM)
    dma = pltpu.SemaphoreType.DMA
    grid = (NX, 8, 8, 32, 128)
    eg, dg = pl.pallas_call(
        functools.partial(kernel, scale),
        out_shape=(
            jax.ShapeDtypeStruct((32, 8192), BF16),
            jax.ShapeDtypeStruct((2, 64, 4096), BF16),
        ),
        in_specs=[hbm] * 6,
        out_specs=(hbm, hbm),
        scratch_shapes=[
            pltpu.VMEM((32, 8192), BF16),
            pltpu.VMEM((2, 64, 4096), BF16),
            dma((3,)),
            pltpu.VMEM((NX, 8, 8, 64, 128), BF16),
            pltpu.VMEM(grid, BF16),
            pltpu.VMEM(grid, BF16),
            pltpu.VMEM((32, 128), BF16),
            pltpu.VMEM((64, 128), BF16),
            pltpu.VMEM((1, 32), F32),
            pltpu.VMEM((1, 64), F32),
            pltpu.VMEM((32, 8192), BF16),
            pltpu.VMEM((2, 64, 4096), BF16),
            pltpu.VMEM((64, 4096), BF16),
            pltpu.VMEM((128, 128), BF16),
            pltpu.VMEM((64, 128), F32),
            pltpu.VMEM((64, 128), F32),
            pltpu.VMEM((32, 128), F32),
            pltpu.VMEM(grid, F32),
            pltpu.VMEM((2, 2, 4, 8, 32, 128), BF16),
            pltpu.VMEM((2, 2, 4, 8, 32, 128), BF16),
            pltpu.VMEM((2, 8, 32, 128), BF16),
            pltpu.VMEM((2, 8, 32, 128), BF16),
            dma((5,)),
            dma((2,)),
            dma((2, 3)),
            dma((2,)),
            dma((2, 2, 2, 4, max(PIECES))),
            dma((4,)),
            dma((4,)),
            dma,
            dma((2, 2, 4, 3)),
            dma,
            dma,
        ],
        compiler_params=pltpu.CompilerParams(collective_id=0, has_side_effects=True),
    )(inputs[0].T, targets[0].T, enc_w[0], enc_b, dec_w[0], dec_b)
    return eg[None], dg[None]


def solution(mesh):
    return jax.shard_map(
        on_device,
        mesh=mesh,
        in_specs=(
            P("section", None, "feat"),
            P("section", None, "feat"),
            P("section", "feat", None),
            P("section", "feat"),
            P("section", None, "feat", None),
            P("section", "feat"),
        ),
        out_specs=(P("section", "feat", None), P("section", None, "feat", None)),
        check_vma=False,
    )
```

time: 101 us -> 92.7 us (0.918)
  Pallas kernels: 96.8 us -> 88.9 us
    pallas_call x1, Pallas kernels: 96.8 us -> 88.9 us  [on_device(): pl.pallas_call(functools.partial(kernel, scale), out_shape=(jax.ShapeDtyp...]
where the time goes in v2:
time: 92.7 us; the launch traced here: 92.4 us
  Pallas kernels  88.9 us (96%)
  local copies, waits for them, and re-layouts  2.93 us (3%)
    pallas_call x1, Pallas kernels, on_device(): pl.pallas_call(functools.partial(kernel, scale), out_shape=(jax.ShapeDtyp...  88.9 us
    unnamed x4, local copies, waits for them, and re-layouts  2.93 us

profile of v2, /device:TPU:1, one launch (start us, length us, event | category | flops | bytes accessed | tf_op | source)
XLA Modules:
  0.0 92.4 jit_solution(9378251061985614638)
XLA Ops:
  0.6 88.9 %shard_map.77 = (bf16[32,8192]{1,0:T(8,128)(2,1)}, bf16[2,64,4096]{2,1,0:T(8,128)(2,1)}) custom-call(bf16[64,128]{1,0:T(8,128)(2,1)} %bitcast.14, bf16[64,128]{1,0:T(8,128)(2,1)} %bitcast.15, bf16[32,8192]{1,0:T(8,128)(2,1)} %bitcast.13, f32[1,32]{1,0:T(1,128)} %encb_hbm.1, bf16[2,64,4096]{2,1,0:T(8,128)(2,1)} %bitcast.10, f32[1,64]{1,0:T(1,128)} %decb_hbm.1), custom_call_target="tpu_custom_call" | custom-call | tf_op jit(solution)/shard_map/pallas_call | solution.py:362
  89.5 0.0 copy-start
  89.5 2.0 %copy.10 = bf16[1,32,8192]{2,1,0:T(8,128)(2,1)} copy(bf16[1,32,8192]{2,1,0:T(8,128)(2,1)} %bitcast.12) | data formatting | bytes 1048576
  91.5 0.0 copy-done
  91.5 1.0 %copy.11 = bf16[1,2,64,4096]{3,2,1,0:T(8,128)(2,1)} copy(bf16[1,2,64,4096]{3,2,1,0:T(8,128)(2,1)S(1)} %bitcast.11) | data formatting | bytes 2097152
Async XLA Ops:
  89.5 2.0 %copy-start = (bf16[2,64,4096]{2,1,0:T(8,128)(2,1)S(1)}, bf16[2,64,4096]{2,1,0:T(8,128)(2,1)}, u32[]{:S(2)}) copy-start(bf16[2,64,4096]{2,1,0:T(8,128)(2,1)} %get-tuple-element.5) | copy-start | bytes 3145732

commit v3 on v2

--- a/solution.py
+++ b/solution.py
@@ -50,22 +50,18 @@
     return [o for o in GROUPS[n] if k <= reach(d, o)]
 
 
-PIECES = (4, 4)
-
-
-def ring_order(g):
-    pieces = PIECES[g]
-    return [
-        (k, h, role, d)
-        for k in range(1, 5) for h in range(pieces) for role in range(2) for d in range(2)
-        if k < 4 or h // (pieces // 2) == d
-    ]
+PIECES = (2, 2)
+LEVELS = (2, 1, 3, 4)
+
+
+def carries(g, k, h, d):
+    return k < 4 or (d == 0 if PIECES[g] == 1 else h // (PIECES[g] // 2) == d)
 
 
 def kernel(
     scale, in_hbm, tgt_hbm, encw_hbm, encb_hbm, decw_hbm, decb_hbm,
     eg_hbm, dg_hbm,
-    eg_ref, dg_ref, out_sem, gin, cod, cprev, cown, tgt, encb_ref, decb_ref, encw, decw, dwn, err, rprev, rsend, active, part, ring_in, ring_out, two_in, two_out,
+    eg_ref, dg_ref, out_sem, gin, cod, cprev, cown, tgt, encb_ref, decb_ref, encw, decw, dwn, err, rprev, sums, encp, wt, wp, active, part, ring_in, ring_out, two_in, two_out,
     load_sem, s_line, r_one, s_ring, r_ring, s_sec, r_sec, s_red, r_red, s_two, r_two,
 ):
     s = lax.axis_index("section")
@@ -133,89 +129,142 @@
     def place(buf, role, i, o):
         return buf.at[colour[role], ring[role][i], line[role][o]]
 
-    def gather(buf, g, src):
+    def gather(buf, g, src, meanwhile):
         own = place(buf, 0, 0, 0)
         pltpu.make_async_copy(src, own, r_one.at[g, 0]).start()
         remote(src, own, s_line.at[g], r_one.at[g, 2], mate).start()
         for o in reversed(OFFS):
             if o != 0:
                 remote(src, own, s_line.at[g], r_one.at[g, 0], along_ring(1, o, xl)).start()
+        meanwhile(-2)
         other = place(buf, 1, 0, 0)
         arrived(other, r_one.at[g, 2])
         for o in reversed(OFFS):
             if o != 0:
                 remote(other, other, s_line.at[g], r_one.at[g, 1], along_ring(0, o, xl)).start()
 
-    def gather_rest(buf, g):
+    def gather_rest(buf, g, meanwhile):
+        meanwhile(-1)
         blocks = 8 // PIECES[g]
 
         def piece(role, i, h):
             return buf.at[colour[role], ring[role][i], pl.ds(h * blocks, blocks)]
 
         def send(role, d, k, h):
-            ref = piece(role, 1 - k if d == 0 else k - 1, h)
-            to = along_ring(role, 1 if d == 0 else -1, xl)
+            way = 1 if d == 0 else -1
+            ref = piece(role, 0 if k < 3 else -2 * way, h)
+            to = along_ring(role, way if k in (1, 3) else 2 * way, xl)
             remote(ref, ref, s_ring.at[g], r_ring.at[g, role, d, k - 1, h], to).start()
 
         for role in range(2):
             arrived(buf.at[0, 0, pl.ds(0, 8 - role)], r_one.at[g, role])
+            for k in (2, 1):
+                for h in range(PIECES[g]):
+                    for d in range(2):
+                        send(role, d, k, h)
+        meanwhile(0)
+        for k in LEVELS:
             for h in range(PIECES[g]):
-                for d in range(2):
-                    send(role, d, 1, h)
-        for k, h, role, d in ring_order(g):
-            arrived(piece(role, -k if d == 0 else k, h), r_ring.at[g, role, d, k - 1, h])
-            if (k + 1, h, role, d) in ring_order(g):
-                send(role, d, k + 1, h)
+                for role in range(2):
+                    for d in range(2):
+                        if carries(g, k, h, d):
+                            arrived(piece(role, -k if d == 0 else k, h), r_ring.at[g, role, d, k - 1, h])
+                        if k == 2:
+                            for further in (4, 3):
+                                if carries(g, further, h, d):
+                                    send(role, d, further, h)
+            meanwhile(k)
 
     def rows_of(buf, i):
         both = jnp.stack([buf[0, i], buf[1, :, i]], axis=1)
         return both.reshape(-1, 128)
 
-    gather(gin, 0, in_hbm)
-    load_d.wait()
     send_w = remote(decw.at[1], dwn, s_sec.at[0], r_sec.at[0], down)
 
-    @pl.when(has_down)
-    def _():
-        send_w.start()
-
-    for load in (load_e, load_t, load_b, load_c):
-        load.wait()
-    gather_rest(gin, 0)
-
-    def pre_step(i, acc):
-        return acc + dot(encw[:, pl.ds(pl.multiple_of(i * 1024, 1024), 1024)], rows_of(gin, i))
-
-    pre = lax.fori_loop(0, NY, pre_step, jnp.zeros((32, 128), F32)) + column(encb_ref[...])
+    def at_distance(k):
+        return (k,) if k in (0, 4) else (k, -k)
+
+    def sort_encoder(i, carry):
+        for j in range(4):
+            for c in range(2):
+                halves = []
+                for o in (2 * j, 2 * j + 1):
+                    base = i * 1024 + o * 128 if c == 0 else o * 1024 + i * 128
+                    group = encw[:, pl.ds(pl.multiple_of(base, 128), 128)]
+                    halves.append(group[:, c * 64 : c * 64 + 64])
+                encp[c, i, :, j * 128 : j * 128 + 128] = jnp.concatenate(halves, axis=1)
+        return carry
+
+    def turn_decoders(i, carry):
+        for q in range(4):
+            cols = pl.ds(pl.multiple_of(i * 512 + q * 128, 128), 128)
+            tile = jnp.concatenate([decw[0, :, cols], dwn[:, cols]], axis=0).T
+            for o in range(2):
+                wt[0, i, 2 * q + o] = tile[o * 64 : o * 64 + 32]
+                wt[1, 2 * q + o, i] = tile[o * 64 + 32 : o * 64 + 64]
+        return carry
+
+    def during_inputs(k):
+        if k == -2:
+            load_d.wait()
+            pl.when(has_down)(send_w.start)
+            sums[...] = jnp.zeros_like(sums)
+            active[...] = jnp.zeros_like(active)
+        elif k == -1:
+            for load in (load_e, load_t, load_b, load_c):
+                load.wait()
+            lax.fori_loop(0, 8, sort_encoder, 0)
+        else:
+            acc = active[...]
+            for i in at_distance(k):
+                for role in range(2):
+                    c, r = colour[role], ring[role][i]
+                    acc = acc + dot(encp[c, r], gin[c, r].reshape(512, 128))
+            active[...] = acc
+        if k == LEVELS[0]:
+            pl.when(has_up)(send_w.wait_recv)
+
+            @pl.when(jnp.logical_not(has_up))
+            def _():
+                dwn[...] = jnp.zeros_like(dwn)
+                err[pl.ds(64, 64), :] = jnp.zeros((64, 128), BF16)
+
+        if k in LEVELS[:3]:
+            turn = 3 * LEVELS.index(k)
+            lax.fori_loop(turn, min(turn + 3, 8), turn_decoders, 0)
+
+    def sort_decoders(i, carry):
+        for c in range(2):
+            wp[c, i] = wt[c, i].reshape(256, 128).T
+        return carry
+
+    def during_codes(k):
+        if k == -1:
+            lax.fori_loop(0, 8, sort_decoders, 0)
+        elif k >= 0:
+            acc = sums[...]
+            for i in at_distance(k):
+                for role in range(2):
+                    c, r = colour[role], ring[role][i]
+                    acc = acc + dot(wp[c, r], cod[c, r].reshape(256, 128))
+            sums[...] = acc
+
+    gather(gin, 0, in_hbm, during_inputs)
+    gather_rest(gin, 0, during_inputs)
+
+    pre = active[...] + column(encb_ref[...])
     act = jnp.maximum(pre, 0.0)
     active[...] = act
     cown[...] = (act * act).astype(BF16)
-    gather(cod, 1, cown)
-
-    @pl.when(has_up)
-    def _():
-        send_w.wait_recv()
-
-    @pl.when(jnp.logical_not(has_up))
-    def _():
-        dwn[...] = jnp.zeros_like(dwn)
-        err[pl.ds(64, 64), :] = jnp.zeros((64, 128), BF16)
-
-    gather_rest(cod, 1)
-
-    def through(weights):
-        def step(i, acc):
-            return acc + dot(weights[:, pl.ds(pl.multiple_of(i * 512, 512), 512)], rows_of(cod, i))
-
-        return lax.fori_loop(0, NY, step, jnp.zeros((64, 128), F32))
-
-    send_r = remote(rsend, rprev, s_sec.at[1], r_sec.at[1], up)
+    gather(cod, 1, cown, during_codes)
+    gather_rest(cod, 1, during_codes)
+
+    send_r = remote(sums.at[pl.ds(64, 64)], rprev, s_sec.at[1], r_sec.at[1], up)
     send_c = remote(cod, cprev, s_sec.at[2], r_sec.at[2], up)
     send_e = remote(err.at[pl.ds(0, 64)], err.at[pl.ds(64, 64)], s_sec.at[3], r_sec.at[3], down)
 
     @pl.when(has_up)
     def _():
-        rsend[...] = through(dwn)
         send_r.start()
         send_c.start()
 
@@ -223,7 +272,7 @@
     def _():
         rprev[...] = jnp.zeros_like(rprev)
 
-    total = through(decw.at[0]) + column(decb_ref[...])
+    total = sums[pl.ds(0, 64), :] + column(decb_ref[...])
 
     @pl.when(has_down)
     def _():
@@ -252,17 +301,6 @@
     def _():
         send_e.wait_recv()
 
-    def grad_step(i, carry):
-        cols = pl.ds(pl.multiple_of(i * 512, 512), 512)
-        both = jnp.concatenate([decw[0, :, cols], dwn[:, cols]], axis=0)
-        block = lax.dot_general(both, err[...], (((0,), (0,)), ((), ())), preferred_element_type=F32)
-        block = block.reshape(NZ, NX, 32, 128)
-        part[0, i] = block[:, 0]
-        part[1, :, i] = block[:, 1]
-        return carry
-
-    lax.fori_loop(0, NY, grad_step, 0)
-
     def own_part(c, i, o):
         return part[0, ys[i], zs[o]] if c == 0 else part[1, zs[i], ys[o]]
 
@@ -270,7 +308,13 @@
         step = 1 if d == 0 else -1
         return at(ys[step], z, xl) if c == 0 else at(y, zs[step], xl)
 
+    def grad_slabs(m):
+        for i in at_distance(m):
+            for c, r in ((0, ys[i]), (1, zs[i])):
+                part[c, r] = dot(wt[c, r].reshape(256, 128), err[...]).reshape(8, 32, 128)
+
     for m in (4, 3, 2, 1):
+        grad_slabs(m)
         for n in reversed(range(len(GROUPS))):
             for c in range(2):
                 for d in range(2):
@@ -288,6 +332,7 @@
                             r_red.at[c, d, m - 1, n], ring_to(c, d),
                         ).start()
 
+    grad_slabs(0)
     for n in reversed(range(len(GROUPS))):
         for c in range(2):
             for d in range(2):
@@ -383,7 +428,10 @@
             pltpu.VMEM((64, 4096), BF16),
             pltpu.VMEM((128, 128), BF16),
             pltpu.VMEM((64, 128), F32),
-            pltpu.VMEM((64, 128), F32),
+            pltpu.VMEM((128, 128), F32),
+            pltpu.VMEM((NX, 8, 32, 512), BF16),
+            pltpu.VMEM(grid, BF16),
+            pltpu.VMEM((NX, 8, 128, 256), BF16),
             pltpu.VMEM((32, 128), F32),
             pltpu.VMEM(grid, F32),
             pltpu.VMEM((2, 2, 4, 8, 32, 128), BF16),

time: 92.7 us -> 82.1 us (0.89)
  Pallas kernels: 88.9 us -> 78.1 us
    pallas_call x1, Pallas kernels: 88.9 us -> 78.1 us  [on_device(): pl.pallas_call(functools.partial(kernel, scale), out_shape=(jax.ShapeDtyp...]
where the time goes in v3:
time: 82.1 us; the launch traced here: 81.6 us
  Pallas kernels  78.1 us (95%)
  local copies, waits for them, and re-layouts  2.93 us (4%)
    pallas_call x1, Pallas kernels, on_device(): pl.pallas_call(functools.partial(kernel, scale), out_shape=(jax.ShapeDtyp...  78.1 us
    unnamed x4, local copies, waits for them, and re-layouts  2.93 us

profile of v3, /device:TPU:1, one launch (start us, length us, event | category | flops | bytes accessed | tf_op | source)
XLA Modules:
  0.0 81.6 jit_solution(16070134598906185696)
XLA Ops:
  0.6 78.1 %shard_map.77 = (bf16[32,8192]{1,0:T(8,128)(2,1)}, bf16[2,64,4096]{2,1,0:T(8,128)(2,1)}) custom-call(bf16[64,128]{1,0:T(8,128)(2,1)} %bitcast.14, bf16[64,128]{1,0:T(8,128)(2,1)} %bitcast.15, bf16[32,8192]{1,0:T(8,128)(2,1)} %bitcast.13, f32[1,32]{1,0:T(1,128)} %encb_hbm.1, bf16[2,64,4096]{2,1,0:T(8,128)(2,1)} %bitcast.10, f32[1,64]{1,0:T(1,128)} %decb_hbm.1), custom_call_target="tpu_custom_call" | custom-call | tf_op jit(solution)/shard_map/pallas_call | solution.py:407
  78.7 0.0 copy-start
  78.7 2.0 %copy.10 = bf16[1,32,8192]{2,1,0:T(8,128)(2,1)} copy(bf16[1,32,8192]{2,1,0:T(8,128)(2,1)} %bitcast.12) | data formatting | bytes 1048576
  80.7 0.0 copy-done
  80.7 1.0 %copy.11 = bf16[1,2,64,4096]{3,2,1,0:T(8,128)(2,1)} copy(bf16[1,2,64,4096]{3,2,1,0:T(8,128)(2,1)S(1)} %bitcast.11) | data formatting | bytes 2097152
Async XLA Ops:
  78.7 2.0 %copy-start = (bf16[2,64,4096]{2,1,0:T(8,128)(2,1)S(1)}, bf16[2,64,4096]{2,1,0:T(8,128)(2,1)}, u32[]{:S(2)}) copy-start(bf16[2,64,4096]{2,1,0:T(8,128)(2,1)} %get-tuple-element.5) | copy-start | bytes 3145732

commit v4 on v3

--- a/solution.py
+++ b/solution.py
@@ -50,8 +50,9 @@
     return [o for o in GROUPS[n] if k <= reach(d, o)]
 
 
-PIECES = (2, 2)
-LEVELS = (2, 1, 3, 4)
+PIECES = (4, 2)
+LEVELS = ((1, 2, 3, 4), (2, 1, 3, 4))
+CROSS = (True, True)
 
 
 def carries(g, k, h, d):
@@ -99,6 +100,8 @@
             pl.semaphore_signal(barrier, inc=1, device_id=at(ys[o], z, xl), device_id_type=MESH)
             pl.semaphore_signal(barrier, inc=1, device_id=at(y, zs[o], xl), device_id_type=MESH)
         pl.semaphore_signal(barrier, inc=1, device_id=along_ring(1, o, 1 - xl), device_id_type=MESH)
+        if o != 0:
+            pl.semaphore_signal(barrier, inc=1, device_id=along_ring(0, o, 1 - xl), device_id_type=MESH)
 
     @pl.when(has_up)
     def _():
@@ -116,7 +119,7 @@
     for load in (load_d, load_e, load_t, load_b, load_c):
         load.start()
 
-    pl.semaphore_wait(barrier, 22 + jnp.where(has_up, 1, 0) + jnp.where(has_down, 1, 0))
+    pl.semaphore_wait(barrier, 29 + jnp.where(has_up, 1, 0) + jnp.where(has_down, 1, 0))
 
     def remote(src, dst, ss, rs, to):
         return pltpu.make_async_remote_copy(
@@ -132,6 +135,13 @@
     def gather(buf, g, src, meanwhile):
         own = place(buf, 0, 0, 0)
         pltpu.make_async_copy(src, own, r_one.at[g, 0]).start()
+        if CROSS[g]:
+            for o in reversed(OFFS):
+                remote(src, own, s_line.at[g], r_one.at[g, 1], along_ring(1, o, 1 - xl)).start()
+                if o != 0:
+                    remote(src, own, s_line.at[g], r_one.at[g, 0], along_ring(1, o, xl)).start()
+            meanwhile(-2)
+            return
         remote(src, own, s_line.at[g], r_one.at[g, 2], mate).start()
         for o in reversed(OFFS):
             if o != 0:
@@ -152,23 +162,26 @@
 
         def send(role, d, k, h):
             way = 1 if d == 0 else -1
-            ref = piece(role, 0 if k < 3 else -2 * way, h)
-            to = along_ring(role, way if k in (1, 3) else 2 * way, xl)
+            chain = LEVELS[g][0] == 1
+            ref = piece(role, -2 * way if k > 2 else -way if k == 2 and chain else 0, h)
+            to = along_ring(role, way if k in (1, 3) or k == 2 and chain else 2 * way, xl)
             remote(ref, ref, s_ring.at[g], r_ring.at[g, role, d, k - 1, h], to).start()
 
         for role in range(2):
-            arrived(buf.at[0, 0, pl.ds(0, 8 - role)], r_one.at[g, role])
-            for k in (2, 1):
+            arrived(buf.at[0, 0, pl.ds(0, 8 if CROSS[g] else 8 - role)], r_one.at[g, role])
+            for k in (2, 1) if LEVELS[g][0] == 2 else (1,):
                 for h in range(PIECES[g]):
                     for d in range(2):
                         send(role, d, k, h)
         meanwhile(0)
-        for k in LEVELS:
+        for k in LEVELS[g]:
             for h in range(PIECES[g]):
                 for role in range(2):
                     for d in range(2):
                         if carries(g, k, h, d):
                             arrived(piece(role, -k if d == 0 else k, h), r_ring.at[g, role, d, k - 1, h])
+                        if k == 1 and LEVELS[g][0] == 1:
+                            send(role, d, 2, h)
                         if k == 2:
                             for further in (4, 3):
                                 if carries(g, further, h, d):
@@ -221,7 +234,7 @@
                     c, r = colour[role], ring[role][i]
                     acc = acc + dot(encp[c, r], gin[c, r].reshape(512, 128))
             active[...] = acc
-        if k == LEVELS[0]:
+        if k == LEVELS[0][0]:
             pl.when(has_up)(send_w.wait_recv)
 
             @pl.when(jnp.logical_not(has_up))
@@ -229,8 +242,8 @@
                 dwn[...] = jnp.zeros_like(dwn)
                 err[pl.ds(64, 64), :] = jnp.zeros((64, 128), BF16)
 
-        if k in LEVELS[:3]:
-            turn = 3 * LEVELS.index(k)
+        if k in LEVELS[0][:3]:
+            turn = 3 * LEVELS[0].index(k)
             lax.fori_loop(turn, min(turn + 3, 8), turn_decoders, 0)
 
     def sort_decoders(i, carry):
@@ -301,54 +314,62 @@
     def _():
         send_e.wait_recv()
 
-    def own_part(c, i, o):
-        return part[0, ys[i], zs[o]] if c == 0 else part[1, zs[i], ys[o]]
-
-    def ring_to(c, d):
-        step = 1 if d == 0 else -1
-        return at(ys[step], z, xl) if c == 0 else at(y, zs[step], xl)
-
     def grad_slabs(m):
         for i in at_distance(m):
             for c, r in ((0, ys[i]), (1, zs[i])):
                 part[c, r] = dot(wt[c, r].reshape(256, 128), err[...]).reshape(8, 32, 128)
 
-    for m in (4, 3, 2, 1):
-        grad_slabs(m)
-        for n in reversed(range(len(GROUPS))):
-            for c in range(2):
+    def half(h):
+        return pl.ds(4 * h, 4)
+
+    def own_part(c, i, h):
+        return part[c, ys[i] if c == 0 else zs[i], half(h)]
+
+    def send_sum(c, d, k, h, value):
+        way = 1 if d == 0 else -1
+        step = way if k in (1, 3) else 2 * way
+        to = at(ys[step], z, xl) if c == 0 else at(y, zs[step], xl)
+        ring_out[c, d, k - 1, half(h)] = value.astype(BF16)
+        remote(
+            ring_out.at[c, d, k - 1, half(h)], ring_in.at[c, d, k - 1, half(h)], s_red, r_red.at[c, d, k - 1, h], to
+        ).start()
+
+    def got_sum(c, d, k, h):
+        arrived(ring_in.at[c, d, k - 1, half(h)], r_red.at[c, d, k - 1, h])
+        return ring_in[c, d, k - 1, half(h)].astype(F32)
+
+    for k in (4, 3, 1):
+        grad_slabs(k)
+        for c in range(2):
+            for h in range(2):
                 for d in range(2):
-                    passing = travellers(n, d, m + 1)
-                    if passing:
-                        arrived(ring_in.at[c, d, m, pl.ds(0, len(passing))], r_red.at[c, d, m, n])
-                    for o in travellers(n, d, m):
-                        slot = OFFS.index(o)
-                        value = own_part(c, m if d == 0 else -m, o)
-                        if o in passing:
-                            value = value + ring_in[c, d, m, slot].astype(F32)
-                        ring_out[c, d, m - 1, slot] = value.astype(BF16)
-                        remote(
-                            ring_out.at[c, d, m - 1, slot], ring_in.at[c, d, m - 1, slot], s_red,
-                            r_red.at[c, d, m - 1, n], ring_to(c, d),
-                        ).start()
-
-    grad_slabs(0)
-    for n in reversed(range(len(GROUPS))):
+                    if k < 4 or h == d:
+                        send_sum(c, d, k, h, own_part(c, k if d == 0 else -k, h))
+    grad_slabs(2)
+    for h in range(2):
         for c in range(2):
             for d in range(2):
-                arrived(ring_in.at[c, d, 0, pl.ds(0, len(GROUPS[n]))], r_red.at[c, d, 0, n])
-            for o in GROUPS[n]:
-                slot = OFFS.index(o)
-                value = own_part(c, 0, o)
+                value = own_part(c, 2 if d == 0 else -2, h) + got_sum(c, d, 3, h)
+                if h == d:
+                    value = value + got_sum(c, d, 4, h)
+                send_sum(c, d, 2, h, value)
+    grad_slabs(0)
+
+    for c in range(2):
+        for h in range(2):
+            value = own_part(c, 0, h)
+            for k in (1, 2):
                 for d in range(2):
-                    value = value + ring_in[c, d, 0, slot].astype(F32)
-                two_out[c, slot] = value.astype(BF16)
-                to = at(y, zs[o], 0) if c == 0 else at(ys[o], z, 1)
-                send_two = remote(two_out.at[c, slot], two_in.at[xl, OFFS.index(back(o))], s_two, r_two, to)
-                if o != 0:
-                    send_two.start()
-                else:
-                    pl.when(xl != c)(send_two.start)
+                    value = value + got_sum(c, d, k, h)
+            two_out[c, half(h)] = value.astype(BF16)
+        for o in reversed(OFFS):
+            j = zs[o] if c == 0 else ys[o]
+            to = at(y, j, 0) if c == 0 else at(j, z, 1)
+            send_two = remote(two_out.at[c, j], two_in.at[xl, z if c == 0 else y], s_two, r_two, to)
+            if o != 0:
+                send_two.start()
+            else:
+                pl.when(xl != c)(send_two.start)
 
     @pl.when(has_down)
     def _():
@@ -362,10 +383,10 @@
     out_1 = pltpu.make_async_copy(dg_ref.at[1], dg_hbm.at[1], out_sem.at[1])
     out_1.start()
     arrived(cprev.at[0, pl.ds(0, 5), pl.ds(0, 3)], r_two)
-    mine = two_out[xl, 0].astype(F32) + two_in[1 - xl, 0].astype(F32)
+    mine = two_out[xl, line[0][0]].astype(F32) + two_in[1 - xl, line[0][0]].astype(F32)
     for o in OFFS[1:]:
-        slot = OFFS.index(o)
-        mine = mine + two_in[0, slot].astype(F32) + two_in[1, slot].astype(F32)
+        for p in range(2):
+            mine = mine + two_in[p, line[0][o]].astype(F32)
 
     pre_grad = (mine * 2.0 * active[...]).astype(BF16)
 
@@ -446,7 +467,7 @@
             dma((4,)),
             dma((4,)),
             dma,
-            dma((2, 2, 4, 3)),
+            dma((2, 2, 4, 2)),
             dma,
             dma,
         ],

time: 82.1 us -> 78.1 us (0.951)
  Pallas kernels: 78.1 us -> 74.4 us
    pallas_call x1, Pallas kernels: 78.1 us -> 74.4 us  [on_device(): pl.pallas_call(functools.partial(kernel, scale), out_shape=(jax.ShapeDtyp...]
where the time goes in v4:
time: 78.1 us; the launch traced here: 78 us
  Pallas kernels  74.4 us (95%)
  local copies, waits for them, and re-layouts  2.93 us (4%)
    pallas_call x1, Pallas kernels, on_device(): pl.pallas_call(functools.partial(kernel, scale), out_shape=(jax.ShapeDtyp...  74.4 us
    unnamed x4, local copies, waits for them, and re-layouts  2.93 us

profile of v4, /device:TPU:1, one launch (start us, length us, event | category | flops | bytes accessed | tf_op | source)
XLA Modules:
  0.0 78.0 jit_solution(4712531440761881380)
XLA Ops:
  0.6 74.4 %shard_map.77 = (bf16[32,8192]{1,0:T(8,128)(2,1)}, bf16[2,64,4096]{2,1,0:T(8,128)(2,1)}) custom-call(bf16[64,128]{1,0:T(8,128)(2,1)} %bitcast.14, bf16[64,128]{1,0:T(8,128)(2,1)} %bitcast.15, bf16[32,8192]{1,0:T(8,128)(2,1)} %bitcast.13, f32[1,32]{1,0:T(1,128)} %encb_hbm.1, bf16[2,64,4096]{2,1,0:T(8,128)(2,1)} %bitcast.10, f32[1,64]{1,0:T(1,128)} %decb_hbm.1), custom_call_target="tpu_custom_call" | custom-call | tf_op jit(solution)/shard_map/pallas_call | solution.py:428
  75.0 0.0 copy-start
  75.0 2.0 %copy.10 = bf16[1,32,8192]{2,1,0:T(8,128)(2,1)} copy(bf16[1,32,8192]{2,1,0:T(8,128)(2,1)} %bitcast.12) | data formatting | bytes 1048576
  77.0 0.0 copy-done
  77.0 1.0 %copy.11 = bf16[1,2,64,4096]{3,2,1,0:T(8,128)(2,1)} copy(bf16[1,2,64,4096]{3,2,1,0:T(8,128)(2,1)S(1)} %bitcast.11) | data formatting | bytes 2097152
Async XLA Ops:
  75.0 2.0 %copy-start = (bf16[2,64,4096]{2,1,0:T(8,128)(2,1)S(1)}, bf16[2,64,4096]{2,1,0:T(8,128)(2,1)}, u32[]{:S(2)}) copy-start(bf16[2,64,4096]{2,1,0:T(8,128)(2,1)} %get-tuple-element.5) | copy-start | bytes 3145732

commit v5 on v4

--- a/solution.py
+++ b/solution.py
@@ -50,9 +50,8 @@
     return [o for o in GROUPS[n] if k <= reach(d, o)]
 
 
-PIECES = (4, 2)
-LEVELS = ((1, 2, 3, 4), (2, 1, 3, 4))
-CROSS = (True, True)
+PIECES = (2, 2)
+LEVELS = (2, 1, 3, 4)
 
 
 def carries(g, k, h, d):
@@ -62,7 +61,7 @@
 def kernel(
     scale, in_hbm, tgt_hbm, encw_hbm, encb_hbm, decw_hbm, decb_hbm,
     eg_hbm, dg_hbm,
-    eg_ref, dg_ref, out_sem, gin, cod, cprev, cown, tgt, encb_ref, decb_ref, encw, decw, dwn, err, rprev, sums, encp, wt, wp, active, part, ring_in, ring_out, two_in, two_out,
+    eg_ref, dg_ref, out_sem, gin, cod, cprev, cown, tgt, encb_ref, decb_ref, encw, decw, dwn, err, rprev, sums, encp, encr, pre_sum, pre_in, wt, wp, active, part, ring_in, ring_out, two_in, two_out,
     load_sem, s_line, r_one, s_ring, r_ring, s_sec, r_sec, s_red, r_red, s_two, r_two,
 ):
     s = lax.axis_index("section")
@@ -129,59 +128,53 @@
     def arrived(blocks, sem):
         pltpu.make_async_copy(blocks, blocks, sem).wait()
 
-    def place(buf, role, i, o):
+    def place(buf, g, role, i, o):
+        if g == 0:
+            return buf.at[role, (ys, zs)[role][i], (zs, ys)[role][o]]
         return buf.at[colour[role], ring[role][i], line[role][o]]
 
-    def gather(buf, g, src, meanwhile):
-        own = place(buf, 0, 0, 0)
-        pltpu.make_async_copy(src, own, r_one.at[g, 0]).start()
-        if CROSS[g]:
+    def along(g, role, o, xx):
+        if g == 1:
+            return along_ring(role, o, xx)
+        return at(ys[o], z, xx) if role == 0 else at(y, zs[o], xx)
+
+    def gather(buf, g, sources):
+        for role, src in enumerate(sources):
+            own = place(buf, g, role, 0, 0)
+            pltpu.make_async_copy(src, own, r_one.at[g, role]).start()
             for o in reversed(OFFS):
-                remote(src, own, s_line.at[g], r_one.at[g, 1], along_ring(1, o, 1 - xl)).start()
+                if g == 1:
+                    remote(src, own, s_line.at[g], r_one.at[g, 1], along(g, 1, o, 1 - xl)).start()
                 if o != 0:
-                    remote(src, own, s_line.at[g], r_one.at[g, 0], along_ring(1, o, xl)).start()
-            meanwhile(-2)
-            return
-        remote(src, own, s_line.at[g], r_one.at[g, 2], mate).start()
-        for o in reversed(OFFS):
-            if o != 0:
-                remote(src, own, s_line.at[g], r_one.at[g, 0], along_ring(1, o, xl)).start()
-        meanwhile(-2)
-        other = place(buf, 1, 0, 0)
-        arrived(other, r_one.at[g, 2])
-        for o in reversed(OFFS):
-            if o != 0:
-                remote(other, other, s_line.at[g], r_one.at[g, 1], along_ring(0, o, xl)).start()
+                    remote(src, own, s_line.at[g], r_one.at[g, role], along(g, 1 - role, o, xl)).start()
 
     def gather_rest(buf, g, meanwhile):
         meanwhile(-1)
         blocks = 8 // PIECES[g]
 
         def piece(role, i, h):
-            return buf.at[colour[role], ring[role][i], pl.ds(h * blocks, blocks)]
+            c, at_ring = (role, (ys, zs)[role]) if g == 0 else (colour[role], ring[role])
+            return buf.at[c, at_ring[i], pl.ds(h * blocks, blocks)]
 
         def send(role, d, k, h):
             way = 1 if d == 0 else -1
-            chain = LEVELS[g][0] == 1
-            ref = piece(role, -2 * way if k > 2 else -way if k == 2 and chain else 0, h)
-            to = along_ring(role, way if k in (1, 3) or k == 2 and chain else 2 * way, xl)
+            ref = piece(role, 0 if k < 3 else -2 * way, h)
+            to = along(g, role, way if k in (1, 3) else 2 * way, xl)
             remote(ref, ref, s_ring.at[g], r_ring.at[g, role, d, k - 1, h], to).start()
 
         for role in range(2):
-            arrived(buf.at[0, 0, pl.ds(0, 8 if CROSS[g] else 8 - role)], r_one.at[g, role])
-            for k in (2, 1) if LEVELS[g][0] == 2 else (1,):
+            arrived(buf.at[0, 0], r_one.at[g, role])
+            for k in (2, 1):
                 for h in range(PIECES[g]):
                     for d in range(2):
                         send(role, d, k, h)
         meanwhile(0)
-        for k in LEVELS[g]:
+        for k in LEVELS:
             for h in range(PIECES[g]):
                 for role in range(2):
                     for d in range(2):
                         if carries(g, k, h, d):
                             arrived(piece(role, -k if d == 0 else k, h), r_ring.at[g, role, d, k - 1, h])
-                        if k == 1 and LEVELS[g][0] == 1:
-                            send(role, d, 2, h)
                         if k == 2:
                             for further in (4, 3):
                                 if carries(g, further, h, d):
@@ -189,8 +182,11 @@
             meanwhile(k)
 
     def rows_of(buf, i):
-        both = jnp.stack([buf[0, i], buf[1, :, i]], axis=1)
-        return both.reshape(-1, 128)
+        return jnp.stack([buf[0, i], buf[1, :, i]], axis=1).reshape(-1, 128)
+
+    def input_rows(i):
+        parts = [gin[c, 0, i] if r == 0 else gin[c, 1, :, i] for c in range(2) for r in range(2)]
+        return jnp.stack(parts, axis=1).reshape(-1, 128)
 
     send_w = remote(decw.at[1], dwn, s_sec.at[0], r_sec.at[0], down)
 
@@ -198,14 +194,15 @@
         return (k,) if k in (0, 4) else (k, -k)
 
     def sort_encoder(i, carry):
-        for j in range(4):
-            for c in range(2):
-                halves = []
-                for o in (2 * j, 2 * j + 1):
-                    base = i * 1024 + o * 128 if c == 0 else o * 1024 + i * 128
-                    group = encw[:, pl.ds(pl.multiple_of(base, 128), 128)]
-                    halves.append(group[:, c * 64 : c * 64 + 64])
-                encp[c, i, :, j * 128 : j * 128 + 128] = jnp.concatenate(halves, axis=1)
+        for c in range(2):
+            for r in range(2):
+                for j in range(2):
+                    parts = []
+                    for o in range(4 * j, 4 * j + 4):
+                        base = i * 1024 + o * 128 if r == 0 else o * 1024 + i * 128
+                        first = c * 64 + r * 32
+                        parts.append(encw[:, pl.ds(pl.multiple_of(base, 128), 128)][:, first : first + 32])
+                    encp[c, r, i, :, j * 128 : j * 128 + 128] = jnp.concatenate(parts, axis=1)
         return carry
 
     def turn_decoders(i, carry):
@@ -217,24 +214,31 @@
                 wt[1, 2 * q + o, i] = tile[o * 64 + 32 : o * 64 + 64]
         return carry
 
+    send_p = remote(encp.at[1 - xl], encr, s_sec.at[4], r_sec.at[4], mate)
+    send_s = remote(pre_sum.at[pl.ds(32, 32)], pre_in, s_sec.at[5], r_sec.at[5], mate)
+    send_g = remote(gin.at[xl], gin.at[xl], s_sec.at[6], r_sec.at[6], mate)
+
     def during_inputs(k):
-        if k == -2:
+        if k == -1:
             load_d.wait()
             pl.when(has_down)(send_w.start)
             sums[...] = jnp.zeros_like(sums)
-            active[...] = jnp.zeros_like(active)
-        elif k == -1:
+            pre_sum[...] = jnp.zeros_like(pre_sum)
             for load in (load_e, load_t, load_b, load_c):
                 load.wait()
             lax.fori_loop(0, 8, sort_encoder, 0)
-        else:
-            acc = active[...]
-            for i in at_distance(k):
+            send_p.start()
+        elif k > 0:
+            if k == LEVELS[0]:
+                send_p.wait_recv()
+            acc = pre_sum[...]
+            for i in at_distance(k) + (at_distance(0) if k == LEVELS[0] else ()):
                 for role in range(2):
-                    c, r = colour[role], ring[role][i]
-                    acc = acc + dot(encp[c, r], gin[c, r].reshape(512, 128))
-            active[...] = acc
-        if k == LEVELS[0][0]:
+                    r = (ys, zs)[role][i]
+                    both = jnp.concatenate([encp[xl, role, r], encr[role, r]], axis=0)
+                    acc = acc + dot(both, gin[xl, role, r].reshape(256, 128))
+            pre_sum[...] = acc
+        if k == LEVELS[0]:
             pl.when(has_up)(send_w.wait_recv)
 
             @pl.when(jnp.logical_not(has_up))
@@ -242,8 +246,8 @@
                 dwn[...] = jnp.zeros_like(dwn)
                 err[pl.ds(64, 64), :] = jnp.zeros((64, 128), BF16)
 
-        if k in LEVELS[0][:3]:
-            turn = 3 * LEVELS[0].index(k)
+        if k in LEVELS[:3]:
+            turn = 3 * LEVELS.index(k)
             lax.fori_loop(turn, min(turn + 3, 8), turn_decoders, 0)
 
     def sort_decoders(i, carry):
@@ -255,6 +259,8 @@
         if k == -1:
             lax.fori_loop(0, 8, sort_decoders, 0)
         elif k >= 0:
+            if k == 0:
+                send_g.start()
             acc = sums[...]
             for i in at_distance(k):
                 for role in range(2):
@@ -262,14 +268,16 @@
                     acc = acc + dot(wp[c, r], cod[c, r].reshape(256, 128))
             sums[...] = acc
 
-    gather(gin, 0, in_hbm, during_inputs)
-    gather_rest(gin, 0, during_inputs)
-
-    pre = active[...] + column(encb_ref[...])
+    gather(gin.at[xl], 0, (in_hbm.at[pl.ds(0, 32)], in_hbm.at[pl.ds(32, 32)]))
+    gather_rest(gin.at[xl], 0, during_inputs)
+
+    send_s.start()
+    send_s.wait_recv()
+    pre = pre_sum[pl.ds(0, 32), :] + pre_in[...] + column(encb_ref[...])
     act = jnp.maximum(pre, 0.0)
     active[...] = act
     cown[...] = (act * act).astype(BF16)
-    gather(cod, 1, cown, during_codes)
+    gather(cod, 1, (cown,))
     gather_rest(cod, 1, during_codes)
 
     send_r = remote(sums.at[pl.ds(64, 64)], rprev, s_sec.at[1], r_sec.at[1], up)
@@ -388,10 +396,11 @@
         for p in range(2):
             mine = mine + two_in[p, line[0][o]].astype(F32)
 
+    send_g.wait_recv()
     pre_grad = (mine * 2.0 * active[...]).astype(BF16)
 
     def enc_step(i, carry):
-        block = dot_nt(pre_grad, rows_of(gin, i))
+        block = dot_nt(pre_grad, input_rows(i))
         cols = pl.ds(pl.multiple_of(i * 1024, 1024), 1024)
         eg_ref[:, cols] = block.astype(BF16)
         pltpu.make_async_copy(eg_ref.at[:, cols], eg_hbm.at[:, cols], out_sem.at[2]).start()
@@ -402,9 +411,12 @@
     pltpu.make_async_copy(eg_ref, eg_hbm, out_sem.at[2]).wait()
     out_0.wait()
     out_1.wait()
-    for g, buf in enumerate((gin, cod)):
-        arrived(buf.at[0, pl.ds(0, 5), pl.ds(0, 3)], s_line.at[g])
-        arrived(buf.at[:, pl.ds(0, 7)], s_ring.at[g])
+    arrived(cod.at[:, 0, pl.ds(0, 7)], s_line.at[0])
+    arrived(cod.at[0, pl.ds(0, 5), pl.ds(0, 3)], s_line.at[1])
+    for g in range(2):
+        arrived(cod.at[:, pl.ds(0, 7)], s_ring.at[g])
+    for copy in (send_p, send_s, send_g):
+        copy.wait_send()
     arrived(ring_out.at[:, :, :, pl.ds(0, 7)], s_red)
     arrived(cprev.at[0, pl.ds(0, 5), pl.ds(0, 3)], s_two)
 
@@ -437,7 +449,7 @@
             pltpu.VMEM((32, 8192), BF16),
             pltpu.VMEM((2, 64, 4096), BF16),
             dma((3,)),
-            pltpu.VMEM((NX, 8, 8, 64, 128), BF16),
+            pltpu.VMEM((NX, NX, 8, 8, 32, 128), BF16),
             pltpu.VMEM(grid, BF16),
             pltpu.VMEM(grid, BF16),
             pltpu.VMEM((32, 128), BF16),
@@ -450,7 +462,10 @@
             pltpu.VMEM((128, 128), BF16),
             pltpu.VMEM((64, 128), F32),
             pltpu.VMEM((128, 128), F32),
-            pltpu.VMEM((NX, 8, 32, 512), BF16),
+            pltpu.VMEM((NX, NX, 8, 32, 256), BF16),
+            pltpu.VMEM((NX, 8, 32, 256), BF16),
+            pltpu.VMEM((64, 128), F32),
+            pltpu.VMEM((32, 128), F32),
             pltpu.VMEM(grid, BF16),
             pltpu.VMEM((NX, 8, 128, 256), BF16),
             pltpu.VMEM((32, 128), F32),
@@ -461,11 +476,11 @@
             pltpu.VMEM((2, 8, 32, 128), BF16),
             dma((5,)),
             dma((2,)),
-            dma((2, 3)),
+            dma((2, 2)),
             dma((2,)),
             dma((2, 2, 2, 4, max(PIECES))),
-            dma((4,)),
-            dma((4,)),
+            dma((7,)),
+            dma((7,)),
             dma,
             dma((2, 2, 4, 2)),
             dma,

time: 78.1 us -> 73.3 us (0.939)
  Pallas kernels: 74.4 us -> 69.6 us
    pallas_call x1, Pallas kernels: 74.4 us -> 69.6 us  [on_device(): pl.pallas_call(functools.partial(kernel, scale), out_shape=(jax.ShapeDtyp...]
where the time goes in v5:
time: 73.3 us; the launch traced here: 73.2 us
  Pallas kernels  69.6 us (95%)
  local copies, waits for them, and re-layouts  2.93 us (4%)
    pallas_call x1, Pallas kernels, on_device(): pl.pallas_call(functools.partial(kernel, scale), out_shape=(jax.ShapeDtyp...  69.6 us
    unnamed x4, local copies, waits for them, and re-layouts  2.93 us

profile of v5, /device:TPU:1, one launch (start us, length us, event | category | flops | bytes accessed | tf_op | source)
XLA Modules:
  0.0 73.2 jit_solution(2613255417295419281)
XLA Ops:
  0.6 69.6 %shard_map.77 = (bf16[32,8192]{1,0:T(8,128)(2,1)}, bf16[2,64,4096]{2,1,0:T(8,128)(2,1)}) custom-call(bf16[64,128]{1,0:T(8,128)(2,1)} %bitcast.14, bf16[64,128]{1,0:T(8,128)(2,1)} %bitcast.15, bf16[32,8192]{1,0:T(8,128)(2,1)} %bitcast.13, f32[1,32]{1,0:T(1,128)} %encb_hbm.1, bf16[2,64,4096]{2,1,0:T(8,128)(2,1)} %bitcast.10, f32[1,64]{1,0:T(1,128)} %decb_hbm.1), custom_call_target="tpu_custom_call" | custom-call | tf_op jit(solution)/shard_map/pallas_call | solution.py:440
  70.2 0.0 copy-start
  70.2 2.0 %copy.10 = bf16[1,32,8192]{2,1,0:T(8,128)(2,1)} copy(bf16[1,32,8192]{2,1,0:T(8,128)(2,1)} %bitcast.12) | data formatting | bytes 1048576
  72.2 0.0 copy-done
  72.2 1.0 %copy.11 = bf16[1,2,64,4096]{3,2,1,0:T(8,128)(2,1)} copy(bf16[1,2,64,4096]{3,2,1,0:T(8,128)(2,1)S(1)} %bitcast.11) | data formatting | bytes 2097152
Async XLA Ops:
  70.2 2.0 %copy-start = (bf16[2,64,4096]{2,1,0:T(8,128)(2,1)S(1)}, bf16[2,64,4096]{2,1,0:T(8,128)(2,1)}, u32[]{:S(2)}) copy-start(bf16[2,64,4096]{2,1,0:T(8,128)(2,1)} %get-tuple-element.5) | copy-start | bytes 3145732

commit v6 on v5

--- a/solution.py
+++ b/solution.py
@@ -52,6 +52,10 @@
 
 PIECES = (2, 2)
 LEVELS = (2, 1, 3, 4)
+
+
+def sem_of(k, h, split):
+    return h if k == split else 2 + [n for n in (1, 2, 3, 4) if n != split].index(k)
 
 
 def carries(g, k, h, d):
@@ -160,7 +164,7 @@
             way = 1 if d == 0 else -1
             ref = piece(role, 0 if k < 3 else -2 * way, h)
             to = along(g, role, way if k in (1, 3) else 2 * way, xl)
-            remote(ref, ref, s_ring.at[g], r_ring.at[g, role, d, k - 1, h], to).start()
+            remote(ref, ref, s_ring.at[g], r_ring.at[g, role, d, sem_of(k, h, 2)], to).start()
 
         for role in range(2):
             arrived(buf.at[0, 0], r_one.at[g, role])
@@ -173,8 +177,11 @@
             for h in range(PIECES[g]):
                 for role in range(2):
                     for d in range(2):
-                        if carries(g, k, h, d):
-                            arrived(piece(role, -k if d == 0 else k, h), r_ring.at[g, role, d, k - 1, h])
+                        i = -k if d == 0 else k
+                        if k in (2, 4) and carries(g, k, h, d):
+                            arrived(piece(role, i, h), r_ring.at[g, role, d, sem_of(k, h, 2)])
+                        elif k in (1, 3) and h == 0:
+                            arrived(buf.at[0, 0], r_ring.at[g, role, d, sem_of(k, h, 2)])
                         if k == 2:
                             for further in (4, 3):
                                 if carries(g, further, h, d):
@@ -272,8 +279,9 @@
     gather_rest(gin.at[xl], 0, during_inputs)
 
     send_s.start()
+    pre = pre_sum[pl.ds(0, 32), :] + column(encb_ref[...])
     send_s.wait_recv()
-    pre = pre_sum[pl.ds(0, 32), :] + pre_in[...] + column(encb_ref[...])
+    pre = pre + pre_in[...]
     act = jnp.maximum(pre, 0.0)
     active[...] = act
     cown[...] = (act * act).astype(BF16)
@@ -339,11 +347,14 @@
         to = at(ys[step], z, xl) if c == 0 else at(y, zs[step], xl)
         ring_out[c, d, k - 1, half(h)] = value.astype(BF16)
         remote(
-            ring_out.at[c, d, k - 1, half(h)], ring_in.at[c, d, k - 1, half(h)], s_red, r_red.at[c, d, k - 1, h], to
+            ring_out.at[c, d, k - 1, half(h)], ring_in.at[c, d, k - 1, half(h)], s_red, r_red.at[c, d, sem_of(k, h, 3)], to
         ).start()
 
     def got_sum(c, d, k, h):
-        arrived(ring_in.at[c, d, k - 1, half(h)], r_red.at[c, d, k - 1, h])
+        if k > 2:
+            arrived(ring_in.at[c, d, k - 1, half(h)], r_red.at[c, d, sem_of(k, h, 3)])
+        elif h == 0:
+            arrived(ring_in.at[c, d, k - 1], r_red.at[c, d, sem_of(k, h, 3)])
         return ring_in[c, d, k - 1, half(h)].astype(F32)
 
     for k in (4, 3, 1):
@@ -406,7 +417,7 @@
         pltpu.make_async_copy(eg_ref.at[:, cols], eg_hbm.at[:, cols], out_sem.at[2]).start()
         return carry
 
-    lax.fori_loop(0, NY, enc_step, 0)
+    lax.fori_loop(0, NY, enc_step, 0, unroll=True)
 
     pltpu.make_async_copy(eg_ref, eg_hbm, out_sem.at[2]).wait()
     out_0.wait()
@@ -478,11 +489,11 @@
             dma((2,)),
             dma((2, 2)),
             dma((2,)),
-            dma((2, 2, 2, 4, max(PIECES))),
+            dma((2, 2, 2, 5)),
             dma((7,)),
             dma((7,)),
             dma,
-            dma((2, 2, 4, 2)),
+            dma((2, 2, 5)),
             dma,
             dma,
         ],

time: 73.3 us -> 72.2 us (0.985)
  Pallas kernels: 69.6 us -> 68.4 us
    pallas_call x1, Pallas kernels: 69.6 us -> 68.4 us  [on_device(): pl.pallas_call(functools.partial(kernel, scale), out_shape=(jax.ShapeDtyp...]
where the time goes in v6:
time: 72.2 us; the launch traced here: 72 us
  Pallas kernels  68.4 us (95%)
  local copies, waits for them, and re-layouts  2.93 us (4%)
    pallas_call x1, Pallas kernels, on_device(): pl.pallas_call(functools.partial(kernel, scale), out_shape=(jax.ShapeDtyp...  68.4 us
    unnamed x4, local copies, waits for them, and re-layouts  2.93 us

profile of v6, /device:TPU:1, one launch (start us, length us, event | category | flops | bytes accessed | tf_op | source)
XLA Modules:
  0.0 72.0 jit_solution(2559848008616832166)
XLA Ops:
  0.6 68.4 %shard_map.77 = (bf16[32,8192]{1,0:T(8,128)(2,1)}, bf16[2,64,4096]{2,1,0:T(8,128)(2,1)}) custom-call(bf16[64,128]{1,0:T(8,128)(2,1)} %bitcast.14, bf16[64,128]{1,0:T(8,128)(2,1)} %bitcast.15, bf16[32,8192]{1,0:T(8,128)(2,1)} %bitcast.13, f32[1,32]{1,0:T(1,128)} %encb_hbm.1, bf16[2,64,4096]{2,1,0:T(8,128)(2,1)} %bitcast.10, f32[1,64]{1,0:T(1,128)} %decb_hbm.1), custom_call_target="tpu_custom_call" | custom-call | tf_op jit(solution)/shard_map/pallas_call | solution.py:451
  69.1 0.0 copy-start
  69.1 2.0 %copy.10 = bf16[1,32,8192]{2,1,0:T(8,128)(2,1)} copy(bf16[1,32,8192]{2,1,0:T(8,128)(2,1)} %bitcast.12) | data formatting | bytes 1048576
  71.0 0.0 copy-done
  71.0 1.0 %copy.11 = bf16[1,2,64,4096]{3,2,1,0:T(8,128)(2,1)} copy(bf16[1,2,64,4096]{3,2,1,0:T(8,128)(2,1)S(1)} %bitcast.11) | data formatting | bytes 2097152
Async XLA Ops:
  69.1 2.0 %copy-start = (bf16[2,64,4096]{2,1,0:T(8,128)(2,1)S(1)}, bf16[2,64,4096]{2,1,0:T(8,128)(2,1)}, u32[]{:S(2)}) copy-start(bf16[2,64,4096]{2,1,0:T(8,128)(2,1)} %get-tuple-element.5) | copy-start | bytes 3145732

commit v7 on v6

--- a/solution.py
+++ b/solution.py
@@ -322,9 +322,6 @@
 
         lax.fori_loop(0, NY, step, 0)
 
-    decoder_grad(0, cod)
-    out_0 = pltpu.make_async_copy(dg_ref.at[0], dg_hbm.at[0], out_sem.at[0])
-    out_0.start()
 
     @pl.when(has_up)
     def _():
@@ -365,6 +362,9 @@
                     if k < 4 or h == d:
                         send_sum(c, d, k, h, own_part(c, k if d == 0 else -k, h))
     grad_slabs(2)
+    decoder_grad(0, cod)
+    out_0 = pltpu.make_async_copy(dg_ref.at[0], dg_hbm.at[0], out_sem.at[0])
+    out_0.start()
     for h in range(2):
         for c in range(2):
             for d in range(2):

time: 72.2 us -> 72.2 us (level)
  no operation moved by 1% of the time
where the time goes in v7:
time: 72.2 us; the launch traced here: 72 us
  Pallas kernels  68.4 us (95%)
  local copies, waits for them, and re-layouts  2.93 us (4%)
    pallas_call x1, Pallas kernels, on_device(): pl.pallas_call(functools.partial(kernel, scale), out_shape=(jax.ShapeDtyp...  68.4 us
    unnamed x4, local copies, waits for them, and re-layouts  2.93 us

profile of v7, /device:TPU:1, one launch (start us, length us, event | category | flops | bytes accessed | tf_op | source)
XLA Modules:
  0.0 72.0 jit_solution(7455698650136646266)
XLA Ops:
  0.6 68.4 %shard_map.77 = (bf16[32,8192]{1,0:T(8,128)(2,1)}, bf16[2,64,4096]{2,1,0:T(8,128)(2,1)}) custom-call(bf16[64,128]{1,0:T(8,128)(2,1)} %bitcast.14, bf16[64,128]{1,0:T(8,128)(2,1)} %bitcast.15, bf16[32,8192]{1,0:T(8,128)(2,1)} %bitcast.13, f32[1,32]{1,0:T(1,128)} %encb_hbm.1, bf16[2,64,4096]{2,1,0:T(8,128)(2,1)} %bitcast.10, f32[1,64]{1,0:T(1,128)} %decb_hbm.1), custom_call_target="tpu_custom_call" | custom-call | tf_op jit(solution)/shard_map/pallas_call | solution.py:451
  69.1 0.0 copy-start
  69.1 2.0 %copy.10 = bf16[1,32,8192]{2,1,0:T(8,128)(2,1)} copy(bf16[1,32,8192]{2,1,0:T(8,128)(2,1)} %bitcast.12) | data formatting | bytes 1048576
  71.0 0.0 copy-done
  71.0 1.0 %copy.11 = bf16[1,2,64,4096]{3,2,1,0:T(8,128)(2,1)} copy(bf16[1,2,64,4096]{3,2,1,0:T(8,128)(2,1)S(1)} %bitcast.11) | data formatting | bytes 2097152
Async XLA Ops:
  69.1 2.0 %copy-start = (bf16[2,64,4096]{2,1,0:T(8,128)(2,1)S(1)}, bf16[2,64,4096]{2,1,0:T(8,128)(2,1)}, u32[]{:S(2)}) copy-start(bf16[2,64,4096]{2,1,0:T(8,128)(2,1)} %get-tuple-element.5) | copy-start | bytes 3145732
